TPU v7x, 256 devices: a whole 4x4x8 slice. The times are simulated.
256 devices in a mesh: band: 8 (over x_lo, y), sector: 32 (over x_hi, z, core).
Axes of the slice: x: 4 (x_hi: 2, x_lo: 2; x = x_hi * 2 + x_lo), y: 4, z: 8, core: 2. Of those that a mesh axis runs over, the one named last changes fastest.
Arguments:
- grid_lat: bfloat16 [64, 2048, 512], P('band', 'sector'), may hold values from -6 to 6
- mesh_lat: bfloat16 [32768, 512], P(('band', 'sector')), may hold values from -6 to 6
- edge_feat: bfloat16 [393216, 512], P(('band', 'sector')), may hold values from -24 to 24
- edge_src: int32 [393216], P(('band', 'sector')), may hold values from 0 to 255, as said below
- edge_dst: int32 [393216], P(('band', 'sector')), may hold values from 0 to 511, as said below
- send_rows: int32 [32768], P(('band', 'sector')), may hold values from 0 to 127
- w_edge1: bfloat16 [1536, 512], replicated, may hold values from -0.15625 to 0.15625
- w_edge2: bfloat16 [512, 512], replicated, may hold values from -0.25 to 0.25
- edge_gain: float32 [512], replicated, may hold values from 0.25 to 1.75
- w_node1: bfloat16 [1024, 512], replicated, may hold values from -0.1875 to 0.1875
- w_node2: bfloat16 [512, 512], replicated, may hold values from -0.25 to 0.25
- node_gain: float32 [512], replicated, may hold values from 0.25 to 1.75
- cotangent: bfloat16 [64, 2048, 512], P('band', 'sector'), may hold values from -6 to 6
Outputs:
- grid_out: bfloat16 [64, 2048, 512], P('band', 'sector')
- grad_grid: bfloat16 [64, 2048, 512], P('band', 'sector')
- grad_mesh: bfloat16 [32768, 512], P(('band', 'sector'))
- grad_w_edge1: float32 [1536, 512], P('sector')
Inputs may be any that keep to these rules, and one draw needn't show every extreme that they name: `edge_src`: A device's mesh table is its 128 own rows followed by 32 rows each from the sector neighbour below, the sector neighbour above, the band neighbour below and the band neighbour above; devices of the first band never read the rows from below, those of the last band never the rows from above. `edge_dst`: each grid point of a device is the destination of exactly 3 of that device's edges; edges are in no particular order.
All inputs are finite; a program needn't handle non-finite values.
Results may differ from a plain program's by a relative error of at most 0.02.
Values may be sent and summed in bfloat16 or wider, within the bound.
No kernel may reach another device: no remote copies, remote signals or barrier semaphores. Data moves between devices by JAX's collectives and lax.ppermute only.
A program may use at most 64 MiB of HBM per device.

v0:
```python
import math
import jax
import jax.numpy as jnp
from jax import lax
from jax.sharding import PartitionSpec as P

EPSILON = 1e-05


def with_halo(shard, sides, width, wrap):
    for axis, dim in sides:
        devices, length = (lax.axis_size(axis), shard.shape[dim])
        up = [(i, (i + 1) % devices) for i in range(devices if wrap else devices - 1)]
        down = [(j, i) for i, j in up]
        last = lax.slice_in_dim(shard, length - width, length, axis=dim)
        initial = lax.slice_in_dim(shard, 0, width, axis=dim)
        before = lax.ppermute(last, axis, up)
        after = lax.ppermute(initial, axis, down)
        shard = jnp.concatenate([before, shard, after], axis=dim)
    return shard


def swish(values):
    return values * jax.nn.sigmoid(values)


def layer_norm(values, gain_vector):
    average = jnp.mean(values, axis=-1, keepdims=True)
    centred = values - average
    spread = jnp.mean(centred * centred, axis=-1, keepdims=True)
    return centred * lax.rsqrt(spread + EPSILON) * gain_vector


def decode_tail(pre_act, grid_wide, edge_dst, w_edge2, edge_gain, w_node1, w_node2, node_gain):
    hidden = swish(pre_act).astype(jnp.bfloat16)
    edge_raw = jnp.dot(hidden, w_edge2, preferred_element_type=jnp.float32)
    message = layer_norm(edge_raw, edge_gain).astype(jnp.bfloat16)
    points = grid_wide.shape[0]
    onehot = (edge_dst[None, :] == jnp.arange(points, dtype=jnp.int32)[:, None]).astype(
        jnp.bfloat16
    )
    aggregated = jnp.dot(onehot, message, preferred_element_type=jnp.float32).astype(jnp.bfloat16)
    node_input = jnp.concatenate([aggregated, grid_wide.astype(jnp.bfloat16)], axis=1)
    node_hidden = swish(jnp.dot(node_input, w_node1, preferred_element_type=jnp.float32)).astype(
        jnp.bfloat16
    )
    node_raw = jnp.dot(node_hidden, w_node2, preferred_element_type=jnp.float32)
    return (grid_wide + layer_norm(node_raw, node_gain)).astype(jnp.bfloat16)


def shards(
    grid_lat,
    mesh_lat,
    edge_feat,
    edge_src,
    edge_dst,
    send_rows,
    w_edge1,
    w_edge2,
    edge_gain,
    w_node1,
    w_node2,
    node_gain,
    cotangent,
):
    feature_width = w_edge2.shape[0]
    lat_rows = grid_lat.shape[0]
    lon_cols = grid_lat.shape[1]
    grid_block = grid_lat.reshape(lat_rows * lon_cols, feature_width)
    cot_block = cotangent.reshape(lat_rows * lon_cols, feature_width)
    own_rows = mesh_lat.shape[0]
    margin = send_rows.shape[0] // 4
    picked = jnp.take(mesh_lat, send_rows, axis=0)
    sector_recv = with_halo(picked[: 2 * margin], (("sector", 0),), margin, True)
    band_recv = with_halo(picked[2 * margin :], (("band", 0),), margin, False)
    mesh_table = jnp.concatenate(
        [
            mesh_lat,
            sector_recv[:margin],
            sector_recv[3 * margin :],
            band_recv[:margin],
            band_recv[3 * margin :],
        ],
        axis=0,
    )
    inputs = jnp.concatenate([edge_feat, mesh_table[edge_src], grid_block[edge_dst]], axis=1)
    pre_act = jnp.dot(inputs, w_edge1, preferred_element_type=jnp.float32)
    grid_wide = grid_block.astype(jnp.float32)

    def finish(pre_values, grid_values):
        return decode_tail(
            pre_values, grid_values, edge_dst, w_edge2, edge_gain, w_node1, w_node2, node_gain
        )

    result, pullback = jax.vjp(finish, pre_act, grid_wide)
    grad_pre, grad_tail = pullback(cot_block)
    grad_pre_b = grad_pre.astype(jnp.bfloat16)
    grad_inputs = lax.dot_general(
        grad_pre_b,
        w_edge1[feature_width:],
        (((1,), (1,)), ((), ())),
        preferred_element_type=jnp.float32,
    )
    grad_table = jax.ops.segment_sum(
        grad_inputs[:, :feature_width], edge_src, num_segments=mesh_table.shape[0]
    )
    grad_grid = grad_tail + jax.ops.segment_sum(
        grad_inputs[:, feature_width:], edge_dst, num_segments=grid_block.shape[0]
    )
    sector_back = with_halo(
        grad_table[own_rows : own_rows + 2 * margin].astype(jnp.bfloat16),
        (("sector", 0),),
        margin,
        True,
    ).astype(jnp.float32)
    band_back = with_halo(
        grad_table[own_rows + 2 * margin :].astype(jnp.bfloat16), (("band", 0),), margin, False
    ).astype(jnp.float32)
    returned = jnp.concatenate(
        [
            sector_back[:margin],
            sector_back[3 * margin :],
            band_back[:margin],
            band_back[3 * margin :],
        ],
        axis=0,
    )
    grad_mesh = (
        grad_table[:own_rows] + jax.ops.segment_sum(returned, send_rows, num_segments=own_rows)
    ).astype(jnp.bfloat16)
    total_edges = edge_feat.shape[0] * lax.axis_size("band") * lax.axis_size("sector")
    grad_scale = 1.0 / math.sqrt(total_edges)
    rows_out = 3 * feature_width // lax.axis_size("sector")
    full_grad = lax.dot_general(
        inputs, grad_pre_b, (((0,), (0,)), ((), ())), preferred_element_type=jnp.float32
    )
    summed = lax.psum(full_grad, ("band", "sector"))
    share_rows = lax.dynamic_slice_in_dim(summed, lax.axis_index("sector") * rows_out, rows_out, 0)
    grad_w_edge1 = share_rows * grad_scale
    grid_out = result.reshape(lat_rows, lon_cols, feature_width)
    grad_grid_out = grad_grid.astype(jnp.bfloat16).reshape(lat_rows, lon_cols, feature_width)
    return (grid_out, grad_grid_out, grad_mesh, grad_w_edge1)


def solution(mesh):
    in_specs = (
        P("band", "sector", None),
        P(("band", "sector"), None),
        P(("band", "sector"), None),
        P(("band", "sector")),
        P(("band", "sector")),
        P(("band", "sector")),
        P(),
        P(),
        P(),
        P(),
        P(),
        P(),
        P("band", "sector", None),
    )
    out_specs = (
        P("band", "sector", None),
        P("band", "sector", None),
        P(("band", "sector"), None),
        P("sector", None),
    )
    return jax.shard_map(shards, mesh=mesh, in_specs=in_specs, out_specs=out_specs, check_vma=False)
```

profile of v0, /device:TPU:2, one launch (start us, length us, event | category | flops | bytes accessed | tf_op | source)
XLA Modules:
  0.0 343.9 jit_solution(3824243465645055062)
XLA Ops:
  8.7 1.8 gather_fusion
  11.2 6.9 %collective-permute-start.1 = (bf16[32,512]{1,0:T(8,128)(2,1)}, bf16[32,512]{1,0:T(8,128)(2,1)S(1)}, u32[]{:S(2)}, u32[]{:S(2)}) collective-permute-start(bf16[32,512]{1,0:T(8,128)(2,1)} %get-tuple-element.21), channel_id=1, source_target_pairs={{1,0},{2,1},{3,2},{4,3},{5,4},{6,5},{7,6},{8,7},{9,8},{10,9},{11,1... | collective-permute-start | bytes 98312 | tf_op jit(solution)/shard_map/ppermute | solution.py:18
  18.1 3.5 %collective-permute-start.2 = (bf16[32,512]{1,0:T(8,128)(2,1)}, bf16[32,512]{1,0:T(8,128)(2,1)S(1)}, u32[]{:S(2)}, u32[]{:S(2)}) collective-permute-start(bf16[32,512]{1,0:T(8,128)(2,1)} %get-tuple-element.20), channel_id=1, source_target_pairs={{0,32},{32,64},{64,96},{96,128},{128,160},{160,192},{192,224},{1,3... | collective-permute-start | bytes 98312 | tf_op jit(solution)/shard_map/ppermute | solution.py:17
  21.6 4.5 %collective-permute-start.3 = (bf16[32,512]{1,0:T(8,128)(2,1)}, bf16[32,512]{1,0:T(8,128)(2,1)S(1)}, u32[]{:S(2)}, u32[]{:S(2)}) collective-permute-start(bf16[32,512]{1,0:T(8,128)(2,1)} %get-tuple-element.19), channel_id=1, source_target_pairs={{32,0},{64,32},{96,64},{128,96},{160,128},{192,160},{224,192},{33,... | collective-permute-start | bytes 98312 | tf_op jit(solution)/shard_map/ppermute | solution.py:18
  27.0 2.7 constant_dynamic-update-slice_fusion.7
  29.7 4.8 %gather_fusion.2 = bf16[1536,512]{1,0:T(8,128)(2,1)S(1)} fusion(bf16[512,512]{1,0:T(8,128)(2,1)S(1)} %bitcast.21, s32[2048]{0:T(1024)S(1)} %pad_clamp_fusion), kind=kCustom, calls=%fused_computation.2 | custom fusion | bytes 3151872 | tf_op jit(solution)/shard_map/gather | solution.py:86
  34.7 5.4 %gather_fusion.1 = bf16[1536,512]{1,0:T(8,128)(2,1)} fusion(bf16[256,512]{1,0:T(8,128)(2,1)S(1)} %constant_dynamic-update-slice_fusion, s32[2048]{0:T(1024)S(1)} %pad_clamp_fusion.1), kind=kCustom, calls=%fused_computation.1 | custom fusion | bytes 3151872 | tf_op jit(solution)/shard_map/gather | solution.py:86
  40.1 2.8 constant_dynamic-update-slice_fusion.6
  42.9 1.3 constant_dynamic-update-slice_fusion.5
  44.2 4.5 %fusion.69 = f32[1536,512]{1,0:T(8,128)S(1)} fusion(bf16[1536,1536]{1,0:T(8,128)(2,1)} %constant_dynamic-update-slice_fusion.5, bf16[1536,512]{1,0:T(8,128)(2,1)S(1)} %copy-done.10), kind=kOutput, calls=%fused_computation.121 | convolution fusion | flops 2415919104 | bytes 9437184 | tf_op jit(solution)/shard_map/dot_general | solution.py:87
  55.2 1.3 fusion.63
  56.5 3.6 %convolution_convert_fusion = bf16[512,1024]{1,0:T(8,128)(2,1)} fusion(bf16[1024,512]{1,0:T(8,128)(2,1)S(1)} %copy-done, f32[512,512]{1,0:T(8,128)} %copy-done.15, bf16[512,512]{1,0:T(8,128)(2,1)} %param.23, f32[512,512]{1,0:T(8,128)S(1)} %get-tuple-element.7, f32[512]{0:T(512)S(1)} %negate_multiply_fusion.1), kind=kOutput, calls=%fused_computation.39 | convolution fusion | flops 808976384 | bytes 4720640 | tf_op jit(solution)/shard_map/transpose(jvp())/dot_general | solution.py:44
  60.1 3.5 %multiply_reduce_fusion = (f32[1536]{0:T(1024)S(1)}, bf16[1536,512]{0,1:T(8,128)(2,1)S(1)}) fusion(f32[1536,512]{0,1:T(8,128)} %copy-done.2, f32[512]{0:T(512)S(1)} %copy-done.9, f32[1536]{0:T(1024)S(1)} %broadcast_multiply_fusion, bf16[512,1024]{1,0:T(8,128)(2,1)} %convolution_convert_fusion, s32[1536]{0:T(1024)S(1)} %copy-done.8), kind=kOutput, calls=%fused_computation.19 | convolution fusion | flops 810809856 | bytes 5263360 | tf_op jit(solution)/shard_map/transpose(jvp())/dot_general | solution.py:42
  65.7 2.6 fusion.1
  69.5 4.3 %fusion.70 = f32[1536,512]{1,0:T(8,128)} fusion(bf16[1536,1536]{1,0:T(8,128)(2,1)S(1)} %bitcast.26, bf16[1536,512]{1,0:T(8,128)(2,1)S(1)} %fusion.1), kind=kOutput, calls=%fused_computation.122 | convolution fusion | flops 2415919104 | bytes 9437184 | tf_op jit(solution)/shard_map/dot_general | solution.py:134
  73.8 6.2 %fusion.36 = f32[1536,1024]{1,0:T(8,128)} fusion(bf16[1536,512]{1,0:T(8,128)(2,1)} %copy-done.14, bf16[1536,512]{1,0:T(8,128)(2,1)} %param.19), kind=kOutput, calls=%fused_computation.55 | convolution fusion | flops 1610612736 | bytes 8912896 | tf_op jit(solution)/shard_map/dot_general | solution.py:98
  80.0 10.6 %scatter_custom_fusion.1 = f32[256,512]{1,0:T(8,128)S(1)} fusion(s32[1536]{0:T(1024)} %param.16, f32[1536,1024]{1,0:T(8,128)} %fusion.36, f32[]{:T(128)} %constant.22.clone.1), kind=kCustom, calls=%fused_computation.13 | custom fusion | flops 786432 | bytes 3670528 | tf_op jit(solution)/shard_map/scatter-add | solution.py:104
  90.6 3.7 %collective-permute-start.7 = (bf16[32,512]{1,0:T(8,128)(2,1)S(1)}, bf16[32,512]{1,0:T(8,128)(2,1)S(1)}, u32[]{:S(2)}, u32[]{:S(2)}) collective-permute-start(bf16[32,512]{1,0:T(8,128)(2,1)S(1)} %get-tuple-element.10), channel_id=1, source_target_pairs={{32,0},{64,32},{96,64},{128,96},{160,128},{192,160},{224,192},{33,... | collective-permute-start | bytes 98312 | tf_op jit(solution)/shard_map/ppermute | solution.py:18
  94.3 2.2 collective-permute-start.6
  97.7 10.9 %scatter_custom_fusion = f32[512,512]{1,0:T(8,128)S(1)} fusion(f32[512,512]{1,0:T(8,128)S(1)} %convert_add_fusion, s32[1536]{0:T(1024)S(1)} %copy-done.8, f32[1536,1024]{1,0:T(8,128)} %fusion.36), kind=kCustom, calls=%fused_computation.15 | custom fusion | flops 786432 | bytes 4194304 | tf_op jit(solution)/shard_map/scatter-add | solution.py:107
  111.1 5.4 %collective-permute-done.4 = bf16[32,512]{1,0:T(8,128)(2,1)S(1)} collective-permute-done((bf16[32,512]{1,0:T(8,128)(2,1)S(1)}, bf16[32,512]{1,0:T(8,128)(2,1)S(1)}, u32[]{:S(2)}, u32[]{:S(2)}) %collective-permute-start.4) | collective-permute-done | bytes 32800 | tf_op jit(solution)/shard_map/ppermute | solution.py:17
  116.5 1.6 scatter_custom_fusion.2
  118.8 216.7 %all-reduce.2.cloned.1.call-done = f32[1536,512]{1,0:T(8,128)} async-done(((f32[1536,512]{1,0:T(8,128)}), f32[1536,512]{1,0:T(8,128)}) %all-reduce.2.cloned.1.call-update) | async-done | bytes 3145744 | tf_op jit(solution)/shard_map/psum | solution.py:137
  335.5 1.5 dynamic-slice_multiply_fusion
  (90 shorter events, 17.2 us)
Async XLA Ops:
  7.2 45.1 %copy-start = (bf16[1024,512]{1,0:T(8,128)(2,1)S(1)}, bf16[1024,512]{1,0:T(8,128)(2,1)}, u32[]{:S(2)}) copy-start(bf16[1024,512]{1,0:T(8,128)(2,1)} %param.22) | copy-start | bytes 3145732
  7.2 22.5 %copy-start.6 = (s32[1536]{0:T(1024)S(1)}, s32[1536]{0:T(1024)}, u32[]{:S(2)}) copy-start(s32[1536]{0:T(1024)} %param.16) | copy-start | bytes 18436
  7.2 22.5 %copy-start.7 = (s32[1536]{0:T(1024)S(1)}, s32[1536]{0:T(1024)}, u32[]{:S(2)}) copy-start(s32[1536]{0:T(1024)} %param.17) | copy-start | bytes 18436
  7.2 22.5 %copy-start.1 = (bf16[8,64,512]{2,1,0:T(8,128)(2,1)S(1)}, bf16[8,64,512]{2,1,0:T(8,128)(2,1)}, u32[]{:S(2)}) copy-start(bf16[8,64,512]{2,1,0:T(8,128)(2,1)} %param.13) | copy-start | bytes 1572868
  7.2 328.3 %all-reduce.2.cloned.1.call-start = ((), (), s32[]{:S(2)}) async-start(), calls=%async_computation | async-start | bytes 6291456 | tf_op jit(solution)/shard_map/psum | solution.py:137
  11.2 23.3 %collective-permute-start = (bf16[32,512]{1,0:T(8,128)(2,1)}, bf16[32,512]{1,0:T(8,128)(2,1)S(1)}, u32[]{:S(2)}, u32[]{:S(2)}) collective-permute-start(bf16[32,512]{1,0:T(8,128)(2,1)} %get-tuple-element.22), channel_id=1, source_target_pairs={{0,1},{1,2},{2,3},{3,4},{4,5},{5,6},{6,7},{7,8},{8,9},{9,10},{10,1... | collective-permute-start | bytes 98312 | tf_op jit(solution)/shard_map/ppermute | solution.py:17
  11.2 23.3 %collective-permute-start.1 = (bf16[32,512]{1,0:T(8,128)(2,1)}, bf16[32,512]{1,0:T(8,128)(2,1)S(1)}, u32[]{:S(2)}, u32[]{:S(2)}) collective-permute-start(bf16[32,512]{1,0:T(8,128)(2,1)} %get-tuple-element.21), channel_id=1, source_target_pairs={{1,0},{2,1},{3,2},{4,3},{5,4},{6,5},{7,6},{8,7},{9,8},{10,9},{11,1... | collective-permute-start | bytes 98312 | tf_op jit(solution)/shard_map/ppermute | solution.py:18
  18.1 16.5 %collective-permute-start.2 = (bf16[32,512]{1,0:T(8,128)(2,1)}, bf16[32,512]{1,0:T(8,128)(2,1)S(1)}, u32[]{:S(2)}, u32[]{:S(2)}) collective-permute-start(bf16[32,512]{1,0:T(8,128)(2,1)} %get-tuple-element.20), channel_id=1, source_target_pairs={{0,32},{32,64},{64,96},{96,128},{128,160},{160,192},{192,224},{1,3... | collective-permute-start | bytes 98312 | tf_op jit(solution)/shard_map/ppermute | solution.py:17
  21.6 13.1 %collective-permute-start.3 = (bf16[32,512]{1,0:T(8,128)(2,1)}, bf16[32,512]{1,0:T(8,128)(2,1)S(1)}, u32[]{:S(2)}, u32[]{:S(2)}) collective-permute-start(bf16[32,512]{1,0:T(8,128)(2,1)} %get-tuple-element.19), channel_id=1, source_target_pairs={{32,0},{64,32},{96,64},{128,96},{160,128},{192,160},{224,192},{33,... | collective-permute-start | bytes 98312 | tf_op jit(solution)/shard_map/ppermute | solution.py:18
  40.1 4.1 %copy-start.10 = (bf16[1536,512]{1,0:T(8,128)(2,1)S(1)}, bf16[1536,512]{1,0:T(8,128)(2,1)}, u32[]{:S(2)}) copy-start(bf16[1536,512]{1,0:T(8,128)(2,1)} %param.19) | copy-start | bytes 4718596
  44.2 4.5 %copy-start.12 = (bf16[512,512]{1,0:T(8,128)(2,1)S(1)}, bf16[512,512]{1,0:T(8,128)(2,1)}, u32[]{:S(2)}) copy-start(bf16[512,512]{1,0:T(8,128)(2,1)} %param.20) | copy-start | bytes 1572868
  48.7 1.6 copy-start.16
  50.4 1.9 copy-start.2
  53.3 1.4 copy-start.4
  53.4 1.4 copy-start.5
  60.1 3.5 %copy-start.3 = (f32[1536,512]{0,1:T(8,128)S(1)}, f32[1536,512]{0,1:T(8,128)}, u32[]{:S(2)}) copy-start(f32[1536,512]{0,1:T(8,128)} %copy-done.2) | copy-start | bytes 9437188
  63.6 2.1 copy-start.17
  63.7 5.8 %slice-start = ((s8[4718592]{0:T(1024)(128)(4,1)}), s8[4194304]{0:T(1024)(128)(4,1)S(1)}, s32[]{:S(2)}) async-start(s8[4718592]{0:T(1024)(128)(4,1)} %bitcast.25), calls=%async_computation.1 | async-start | bytes 8388608
  65.7 3.8 %slice-start.1 = ((s8[4718592]{0:T(1024)(128)(4,1)}), s8[524288]{0:T(1024)(128)(4,1)S(1)}, s32[]{:S(2)}) async-start(s8[4718592]{0:T(1024)(128)(4,1)} %bitcast.25), calls=%async_computation.2 | async-start | bytes 1048576
  68.3 1.2 copy-start.14
  90.6 19.4 %collective-permute-start.7 = (bf16[32,512]{1,0:T(8,128)(2,1)S(1)}, bf16[32,512]{1,0:T(8,128)(2,1)S(1)}, u32[]{:S(2)}, u32[]{:S(2)}) collective-permute-start(bf16[32,512]{1,0:T(8,128)(2,1)S(1)} %get-tuple-element.10), channel_id=1, source_target_pairs={{32,0},{64,32},{96,64},{128,96},{160,128},{192,160},{224,192},{33,... | collective-permute-start | bytes 98312 | tf_op jit(solution)/shard_map/ppermute | solution.py:18
  94.3 15.7 %collective-permute-start.6 = (bf16[32,512]{1,0:T(8,128)(2,1)S(1)}, bf16[32,512]{1,0:T(8,128)(2,1)S(1)}, u32[]{:S(2)}, u32[]{:S(2)}) collective-permute-start(bf16[32,512]{1,0:T(8,128)(2,1)S(1)} %get-tuple-element.11), channel_id=1, source_target_pairs={{0,32},{32,64},{64,96},{96,128},{128,160},{160,192},{192,224},{1,3... | collective-permute-start | bytes 98312 | tf_op jit(solution)/shard_map/ppermute | solution.py:17
  109.5 1.6 collective-permute-start.5
  109.5 7.0 %collective-permute-start.4 = (bf16[32,512]{1,0:T(8,128)(2,1)S(1)}, bf16[32,512]{1,0:T(8,128)(2,1)S(1)}, u32[]{:S(2)}, u32[]{:S(2)}) collective-permute-start(bf16[32,512]{1,0:T(8,128)(2,1)S(1)} %get-tuple-element.9), channel_id=1, source_target_pairs={{0,1},{1,2},{2,3},{3,4},{4,5},{5,6},{6,7},{7,8},{8,9},{9,10},{10,1... | collective-permute-start | bytes 98312 | tf_op jit(solution)/shard_map/ppermute | solution.py:17
  (5 other events, 4.5 us)
Sparse Core Ops, SparseCore 0:
  73.9 261.5 all-reduce.1
where the time goes:
time: 344 us
  waiting for transfers between devices  223 us (65%)
  other arithmetic  32 us (9%)
  matrix products  28.2 us (8%)
  local copies, waits for them, and re-layouts  24.8 us (7%)
  starting transfers between devices  21.2 us (6%)
  between operations  14.5 us (4%)
    psum x1, waiting for transfers between devices, shards(): summed = lax.psum(full_grad, ('band', 'sector'))  217 us
    ppermute x4, starting transfers between devices, with_halo(): after = lax.ppermute(initial, axis, down)  15 us
    scatter-add x1, other arithmetic, shards(): jax.ops.segment_sum(grad_inputs[:, feature_width:], edge_dst, num_segment...  10.9 us
    unnamed x46, local copies, waits for them, and re-layouts  10.8 us
    scatter-add x1, other arithmetic, shards(): jax.ops.segment_sum(grad_inputs[:, :feature_width], edge_src, num_segment...  10.6 us
  transfers between devices with their start and end apart: 9, of which 3 were waited for; matrix products, arithmetic and copies ran while one was open for 12% of the time, Pallas kernels for 0%

commit v1 on v0

--- a/solution.py
+++ b/solution.py
@@ -134,7 +134,7 @@
     full_grad = lax.dot_general(
         inputs, grad_pre_b, (((0,), (0,)), ((), ())), preferred_element_type=jnp.float32
     )
-    summed = lax.psum(full_grad, ("band", "sector"))
+    summed = lax.psum(lax.psum(full_grad, "sector"), "band")
     share_rows = lax.dynamic_slice_in_dim(summed, lax.axis_index("sector") * rows_out, rows_out, 0)
     grad_w_edge1 = share_rows * grad_scale
     grid_out = result.reshape(lat_rows, lon_cols, feature_width)

time: 344 us -> 452 us (1.31)
  waiting for transfers between devices: 223 us -> 324 us
  starting transfers between devices: 21.2 us -> 26.8 us
    psum x1 -> x2, waiting for transfers between devices: 217 us -> 317 us  [shards(): summed = lax.psum(lax.psum(full_grad, 'sector'), 'band')]
    ppermute x4, starting transfers between devices: 15 us -> 21.3 us  [with_halo(): after = lax.ppermute(initial, axis, down)]
  transfers between devices with their start and end apart: 9 -> 10, of which waited for: 3 -> 4; matrix products, arithmetic and copies ran while one was open for 12% -> 9% of each run, Pallas kernels for 0% -> 0%
where the time goes in v1:
time: 452 us; the launch traced here: 450 us
  waiting for transfers between devices  324 us (72%)
  other arithmetic  32 us (7%)
  matrix products  28.2 us (6%)
  starting transfers between devices  26.8 us (6%)
  local copies, waits for them, and re-layouts  24.8 us (5%)
  between operations  14.5 us (3%)
    psum x2, waiting for transfers between devices, shards(): summed = lax.psum(lax.psum(full_grad, 'sector'), 'band')  317 us
    ppermute x4, starting transfers between devices, with_halo(): after = lax.ppermute(initial, axis, down)  21.3 us
    scatter-add x1, other arithmetic, shards(): jax.ops.segment_sum(grad_inputs[:, feature_width:], edge_dst, num_segment...  10.9 us
    unnamed x46, local copies, waits for them, and re-layouts  10.8 us
    scatter-add x1, other arithmetic, shards(): jax.ops.segment_sum(grad_inputs[:, :feature_width], edge_src, num_segment...  10.6 us
  transfers between devices with their start and end apart: 10, of which 4 were waited for; matrix products, arithmetic and copies ran while one was open for 9% of the time, Pallas kernels for 0%

profile of v1, /device:TPU:2, one launch (start us, length us, event | category | flops | bytes accessed | tf_op | source)
XLA Modules:
  0.0 450.3 jit_solution(6408935485611180460)
XLA Ops:
  8.7 1.8 gather_fusion
  11.2 6.9 %collective-permute-start.1 = (bf16[32,512]{1,0:T(8,128)(2,1)}, bf16[32,512]{1,0:T(8,128)(2,1)S(1)}, u32[]{:S(2)}, u32[]{:S(2)}) collective-permute-start(bf16[32,512]{1,0:T(8,128)(2,1)} %get-tuple-element.21), channel_id=1, source_target_pairs={{1,0},{2,1},{3,2},{4,3},{5,4},{6,5},{7,6},{8,7},{9,8},{10,9},{11,1... | collective-permute-start | bytes 98312 | tf_op jit(solution)/shard_map/ppermute | solution.py:18
  18.1 3.5 collective-permute-start.2
  21.6 4.5 collective-permute-start.3
  27.0 2.7 constant_dynamic-update-slice_fusion.7
  29.7 4.8 %gather_fusion.2 = bf16[1536,512]{1,0:T(8,128)(2,1)S(1)} fusion(bf16[512,512]{1,0:T(8,128)(2,1)S(1)} %bitcast.21, s32[2048]{0:T(1024)S(1)} %pad_clamp_fusion), kind=kCustom, calls=%fused_computation.2 | custom fusion | bytes 3151872 | tf_op jit(solution)/shard_map/gather | solution.py:86
  34.7 5.4 %gather_fusion.1 = bf16[1536,512]{1,0:T(8,128)(2,1)} fusion(bf16[256,512]{1,0:T(8,128)(2,1)S(1)} %constant_dynamic-update-slice_fusion, s32[2048]{0:T(1024)S(1)} %pad_clamp_fusion.1), kind=kCustom, calls=%fused_computation.1 | custom fusion | bytes 3151872 | tf_op jit(solution)/shard_map/gather | solution.py:86
  40.1 2.8 constant_dynamic-update-slice_fusion.6
  44.2 4.5 fusion.69
  56.5 3.6 convolution_convert_fusion
  60.1 3.5 multiply_reduce_fusion
  65.7 2.6 fusion.1
  69.5 4.3 fusion.70
  73.8 271.0 %all-reduce.3.cloned.1.call-done = f32[1536,512]{1,0:T(8,128)} async-done(((f32[1536,512]{1,0:T(8,128)}), f32[1536,512]{1,0:T(8,128)}) %all-reduce.3.cloned.1.call-update) | async-done | bytes 3145744 | tf_op jit(solution)/shard_map/psum | solution.py:137
  344.9 6.2 %fusion.36 = f32[1536,1024]{1,0:T(8,128)} fusion(bf16[1536,512]{1,0:T(8,128)(2,1)} %copy-done.14, bf16[1536,512]{1,0:T(8,128)(2,1)} %param.19), kind=kOutput, calls=%fused_computation.55 | convolution fusion | flops 1610612736 | bytes 8912896 | tf_op jit(solution)/shard_map/dot_general | solution.py:98
  351.1 10.6 %scatter_custom_fusion.1 = f32[256,512]{1,0:T(8,128)S(1)} fusion(s32[1536]{0:T(1024)} %param.16, f32[1536,1024]{1,0:T(8,128)} %fusion.36, f32[]{:T(128)} %constant.22.clone.1), kind=kCustom, calls=%fused_computation.13 | custom fusion | flops 786432 | bytes 3670528 | tf_op jit(solution)/shard_map/scatter-add | solution.py:104
  361.7 5.2 %collective-permute-start.7 = (bf16[32,512]{1,0:T(8,128)(2,1)S(1)}, bf16[32,512]{1,0:T(8,128)(2,1)S(1)}, u32[]{:S(2)}, u32[]{:S(2)}) collective-permute-start(bf16[32,512]{1,0:T(8,128)(2,1)S(1)} %get-tuple-element.10), channel_id=1, source_target_pairs={{32,0},{64,32},{96,64},{128,96},{160,128},{192,160},{224,192},{33,... | collective-permute-start | bytes 98312 | tf_op jit(solution)/shard_map/ppermute | solution.py:18
  366.9 1.9 collective-permute-start.6
  370.1 10.9 %scatter_custom_fusion = f32[512,512]{1,0:T(8,128)S(1)} fusion(f32[512,512]{1,0:T(8,128)S(1)} %convert_add_fusion, s32[1536]{0:T(1024)S(1)} %copy-done.8, f32[1536,1024]{1,0:T(8,128)} %fusion.36), kind=kCustom, calls=%fused_computation.15 | custom fusion | flops 786432 | bytes 4194304 | tf_op jit(solution)/shard_map/scatter-add | solution.py:107
  381.8 4.8 %collective-permute-start.5 = (bf16[32,512]{1,0:T(8,128)(2,1)S(1)}, bf16[32,512]{1,0:T(8,128)(2,1)S(1)}, u32[]{:S(2)}, u32[]{:S(2)}) collective-permute-start(bf16[32,512]{1,0:T(8,128)(2,1)S(1)} %get-tuple-element.12), channel_id=1, source_target_pairs={{1,0},{2,1},{3,2},{4,3},{5,4},{6,5},{7,6},{8,7},{9,8},{10,9},{11,1... | collective-permute-start | bytes 98312 | tf_op jit(solution)/shard_map/ppermute | solution.py:18
  386.7 1.6 collective-permute-done.5
  388.2 5.5 %collective-permute-done.4 = bf16[32,512]{1,0:T(8,128)(2,1)S(1)} collective-permute-done((bf16[32,512]{1,0:T(8,128)(2,1)S(1)}, bf16[32,512]{1,0:T(8,128)(2,1)S(1)}, u32[]{:S(2)}, u32[]{:S(2)}) %collective-permute-start.4) | collective-permute-done | bytes 32800 | tf_op jit(solution)/shard_map/ppermute | solution.py:17
  393.7 1.6 scatter_custom_fusion.2
  396.0 45.9 %all-reduce.5.cloned.1.call-done = f32[1536,512]{1,0:T(8,128)} async-done(((f32[1536,512]{1,0:T(8,128)}), f32[1536,512]{1,0:T(8,128)}) %all-reduce.5.cloned.1.call-update) | async-done | bytes 3145744 | tf_op jit(solution)/shard_map/psum | solution.py:137
  (93 shorter events, 19.9 us)
Async XLA Ops:
  7.2 45.1 %copy-start = (bf16[1024,512]{1,0:T(8,128)(2,1)S(1)}, bf16[1024,512]{1,0:T(8,128)(2,1)}, u32[]{:S(2)}) copy-start(bf16[1024,512]{1,0:T(8,128)(2,1)} %param.22) | copy-start | bytes 3145732
  7.2 22.5 %copy-start.6 = (s32[1536]{0:T(1024)S(1)}, s32[1536]{0:T(1024)}, u32[]{:S(2)}) copy-start(s32[1536]{0:T(1024)} %param.16) | copy-start | bytes 18436
  7.2 22.5 %copy-start.7 = (s32[1536]{0:T(1024)S(1)}, s32[1536]{0:T(1024)}, u32[]{:S(2)}) copy-start(s32[1536]{0:T(1024)} %param.17) | copy-start | bytes 18436
  7.2 22.5 %copy-start.1 = (bf16[8,64,512]{2,1,0:T(8,128)(2,1)S(1)}, bf16[8,64,512]{2,1,0:T(8,128)(2,1)}, u32[]{:S(2)}) copy-start(bf16[8,64,512]{2,1,0:T(8,128)(2,1)} %param.13) | copy-start | bytes 1572868
  7.2 337.6 %all-reduce.3.cloned.1.call-start = ((), (), s32[]{:S(2)}) async-start(), calls=%async_computation | async-start | bytes 6291456 | tf_op jit(solution)/shard_map/psum | solution.py:137
  11.2 23.3 %collective-permute-start = (bf16[32,512]{1,0:T(8,128)(2,1)}, bf16[32,512]{1,0:T(8,128)(2,1)S(1)}, u32[]{:S(2)}, u32[]{:S(2)}) collective-permute-start(bf16[32,512]{1,0:T(8,128)(2,1)} %get-tuple-element.22), channel_id=1, source_target_pairs={{0,1},{1,2},{2,3},{3,4},{4,5},{5,6},{6,7},{7,8},{8,9},{9,10},{10,1... | collective-permute-start | bytes 98312 | tf_op jit(solution)/shard_map/ppermute | solution.py:17
  11.2 23.3 %collective-permute-start.1 = (bf16[32,512]{1,0:T(8,128)(2,1)}, bf16[32,512]{1,0:T(8,128)(2,1)S(1)}, u32[]{:S(2)}, u32[]{:S(2)}) collective-permute-start(bf16[32,512]{1,0:T(8,128)(2,1)} %get-tuple-element.21), channel_id=1, source_target_pairs={{1,0},{2,1},{3,2},{4,3},{5,4},{6,5},{7,6},{8,7},{9,8},{10,9},{11,1... | collective-permute-start | bytes 98312 | tf_op jit(solution)/shard_map/ppermute | solution.py:18
  18.1 16.5 %collective-permute-start.2 = (bf16[32,512]{1,0:T(8,128)(2,1)}, bf16[32,512]{1,0:T(8,128)(2,1)S(1)}, u32[]{:S(2)}, u32[]{:S(2)}) collective-permute-start(bf16[32,512]{1,0:T(8,128)(2,1)} %get-tuple-element.20), channel_id=1, source_target_pairs={{0,32},{32,64},{64,96},{96,128},{128,160},{160,192},{192,224},{1,3... | collective-permute-start | bytes 98312 | tf_op jit(solution)/shard_map/ppermute | solution.py:17
  21.6 13.1 %collective-permute-start.3 = (bf16[32,512]{1,0:T(8,128)(2,1)}, bf16[32,512]{1,0:T(8,128)(2,1)S(1)}, u32[]{:S(2)}, u32[]{:S(2)}) collective-permute-start(bf16[32,512]{1,0:T(8,128)(2,1)} %get-tuple-element.19), channel_id=1, source_target_pairs={{32,0},{64,32},{96,64},{128,96},{160,128},{192,160},{224,192},{33,... | collective-permute-start | bytes 98312 | tf_op jit(solution)/shard_map/ppermute | solution.py:18
  40.1 4.1 copy-start.10
  44.2 4.5 %copy-start.12 = (bf16[512,512]{1,0:T(8,128)(2,1)S(1)}, bf16[512,512]{1,0:T(8,128)(2,1)}, u32[]{:S(2)}) copy-start(bf16[512,512]{1,0:T(8,128)(2,1)} %param.20) | copy-start | bytes 1572868
  48.7 1.6 copy-start.16
  50.4 1.9 copy-start.2
  53.3 1.4 copy-start.4
  53.4 1.4 copy-start.5
  60.1 3.5 copy-start.3
  63.6 2.1 copy-start.17
  63.7 5.8 %slice-start = ((s8[4718592]{0:T(1024)(128)(4,1)}), s8[4194304]{0:T(1024)(128)(4,1)S(1)}, s32[]{:S(2)}) async-start(s8[4718592]{0:T(1024)(128)(4,1)} %bitcast.25), calls=%async_computation.2 | async-start | bytes 8388608
  65.7 3.8 slice-start.1
  73.8 368.2 %all-reduce.5.cloned.1.call-start = ((), (), s32[]{:S(2)}) async-start(), calls=%async_computation.1 | async-start | bytes 6291456 | tf_op jit(solution)/shard_map/psum | solution.py:137
  361.7 24.9 %collective-permute-start.7 = (bf16[32,512]{1,0:T(8,128)(2,1)S(1)}, bf16[32,512]{1,0:T(8,128)(2,1)S(1)}, u32[]{:S(2)}, u32[]{:S(2)}) collective-permute-start(bf16[32,512]{1,0:T(8,128)(2,1)S(1)} %get-tuple-element.10), channel_id=1, source_target_pairs={{32,0},{64,32},{96,64},{128,96},{160,128},{192,160},{224,192},{33,... | collective-permute-start | bytes 98312 | tf_op jit(solution)/shard_map/ppermute | solution.py:18
  366.9 19.7 %collective-permute-start.6 = (bf16[32,512]{1,0:T(8,128)(2,1)S(1)}, bf16[32,512]{1,0:T(8,128)(2,1)S(1)}, u32[]{:S(2)}, u32[]{:S(2)}) collective-permute-start(bf16[32,512]{1,0:T(8,128)(2,1)S(1)} %get-tuple-element.11), channel_id=1, source_target_pairs={{0,32},{32,64},{64,96},{96,128},{128,160},{160,192},{192,224},{1,3... | collective-permute-start | bytes 98312 | tf_op jit(solution)/shard_map/ppermute | solution.py:17
  381.8 6.4 %collective-permute-start.5 = (bf16[32,512]{1,0:T(8,128)(2,1)S(1)}, bf16[32,512]{1,0:T(8,128)(2,1)S(1)}, u32[]{:S(2)}, u32[]{:S(2)}) collective-permute-start(bf16[32,512]{1,0:T(8,128)(2,1)S(1)} %get-tuple-element.12), channel_id=1, source_target_pairs={{1,0},{2,1},{3,2},{4,3},{5,4},{6,5},{7,6},{8,7},{9,8},{10,9},{11,1... | collective-permute-start | bytes 98312 | tf_op jit(solution)/shard_map/ppermute | solution.py:18
  386.6 7.1 %collective-permute-start.4 = (bf16[32,512]{1,0:T(8,128)(2,1)S(1)}, bf16[32,512]{1,0:T(8,128)(2,1)S(1)}, u32[]{:S(2)}, u32[]{:S(2)}) collective-permute-start(bf16[32,512]{1,0:T(8,128)(2,1)S(1)} %get-tuple-element.9), channel_id=1, source_target_pairs={{0,1},{1,2},{2,3},{3,4},{4,5},{5,6},{6,7},{7,8},{8,9},{9,10},{10,1... | collective-permute-start | bytes 98312 | tf_op jit(solution)/shard_map/ppermute | solution.py:17
  (6 other events, 5.7 us)
Sparse Core Ops, SparseCore 0:
  73.9 270.8 all-reduce.2
  347.7 94.1 all-reduce.4
